TPU v7x, 32 devices: a whole 2x2x4 slice. The times are simulated.
32 devices in a mesh: gx: 2 (over x), gy: 2 (over core), gz: 8 (over z, y).
Axes of the slice: x: 2, y: 2, z: 4, core: 2. Of those that a mesh axis runs over, the one named last changes fastest.
Arguments:
- state: float32 [24, 32, 16, 512], P(None, 'gx', ('gy', 'gz')), may hold values from -6 to 6
- base: float32 [24, 32, 16, 512], P(None, 'gx', ('gy', 'gz')), may hold values from -0.6 to 0.6
- accum: float32 [24, 32, 16, 512], P(None, 'gx', ('gy', 'gz')), may hold values from -0.3 to 0.3
- owner: int32 [8], replicated, may hold values from 0 to 7, each once
Outputs:
- next_section: float32 [24, 32, 16, 512], P(None, 'gx', ('gy', 'gz'))
- accum_out: float32 [24, 32, 16, 512], P(None, 'gx', ('gy', 'gz'))
Inputs may be any that keep to these rules, and one draw needn't show every extreme that they name: owner names every index of gz once.
All inputs are finite; a program needn't handle non-finite values.
Results may differ from a plain program's by a relative error of at most 0.00002.
Values sent between devices are 32-bit elements; how exact they have to be, the bound alone decides.
No kernel may reach another device: no remote copies, remote signals or barrier semaphores. Data moves between devices by JAX's collectives and lax.ppermute only.
A program may use at most 192 MiB of HBM per device.

v0:
```python
import functools

import jax
import jax.numpy as jnp
from jax import lax
from jax.experimental import pallas as pl
from jax.experimental.pallas import tpu as pltpu
from jax.sharding import PartitionSpec as P


BLOCK = 16


DAMPING_STRENGTH = 1.0
SPACING = 1.0
TIME_STEP = 0.25
SECTION_SHIFT = 0.5
SECTION_WEIGHT = 1.0 / 3.0

LANES = 128
GHOST = 3
SLOT = 2 * GHOST
DEPTH = 2 * BLOCK
SLOTS = DEPTH // SLOT
DAMP = DAMPING_STRENGTH / (64.0 * SPACING)
LAPL = 1.0 / (12.0 * SPACING * SPACING)
VMEM = pltpu.VMEM
SMEM = pltpu.SMEM


def vmem_spec():
    return pl.BlockSpec(memory_space=VMEM)


def call(kernel, outs, in_specs, out_specs=None, scratch=(), cost=None, aliases=None):
    multiple = isinstance(outs, (list, tuple))
    if out_specs is None:
        out_specs = [vmem_spec() for _ in outs] if multiple else vmem_spec()
    return pl.pallas_call(
        kernel,
        out_shape=outs,
        in_specs=in_specs,
        out_specs=out_specs,
        scratch_shapes=list(scratch),
        input_output_aliases=aliases or {},
        compiler_params=pltpu.CompilerParams(vmem_limit_bytes=16 * 1024 * 1024),
        cost_estimate=pl.CostEstimate(flops=cost[0], bytes_accessed=cost[1], transcendentals=0),
    )


def lane_index(rows):
    return lax.broadcasted_iota(jnp.int32, (rows, LANES), 1)


def pack_faces_kernel(state_ref, out_ref):
    fields, rows, _ = state_ref.shape
    slot = (lane_index(rows) % DEPTH) // SLOT
    for group in range(out_ref.shape[0]):
        packed = jnp.zeros((rows, LANES), jnp.float32)
        for j in range(min(SLOTS, fields - group * SLOTS)):
            moved = pltpu.roll(state_ref[group * SLOTS + j], GHOST + SLOT * j, 1)
            packed = jnp.where(slot == j, moved, packed)
        out_ref[group] = packed


def pack_ends_kernel(per_layer, state_ref, layers_ref, strips_ref):
    fields, rows, _ = state_ref.shape
    edge = GHOST * per_layer
    layers = rows // per_layer
    layers_ref[:, :edge] = state_ref[:, :edge]
    layers_ref[:, edge:] = state_ref[:, rows - edge :]
    for f in range(fields):
        strips_ref[f, :layers] = state_ref[f, pl.ds(0, layers, stride=per_layer)]
        strips_ref[f, layers:] = state_ref[f, pl.ds(per_layer - 1, layers, stride=per_layer)]


def find_column(owner_ref, device, columns):
    def body(t, found):
        return jnp.where(owner_ref[t] == device, t, found)

    return lax.fori_loop(0, columns, body, jnp.int32(0))


def neighbours(owner_ref, device, columns):
    column = find_column(owner_ref, device, columns)
    below = owner_ref[lax.rem(column + columns - 1, columns)]
    above = owner_ref[lax.rem(column + 1, columns)]
    return below, above


def source_masks(lanes, low_from, high_from, count):
    chosen = jnp.where(lanes, low_from, high_from)
    return [chosen == d for d in range(1, count)]


def forward_kernel(columns, cross, owner_ref, me_ref, *refs):
    *sources, out_ref = refs
    me = me_ref[0]
    below, above = neighbours(owner_ref, me ^ cross, columns)
    low_part = (lane_index(out_ref.shape[1]) % DEPTH) % SLOT < GHOST
    masks = source_masks(low_part, me ^ below, me ^ above, len(sources))
    for g in range(out_ref.shape[0]):
        chosen = sources[0][g]
        for mask, source in zip(masks, sources[1:]):
            chosen = jnp.where(mask, source[g], chosen)
        out_ref[g] = chosen


def field_sums(per_layer, lane, state_ref, strips_ref, f, wide_ref, after_ref, before_ref):
    rows = state_ref.shape[1]
    edge = GHOST * per_layer
    layers = rows // per_layer
    depth = lane % DEPTH
    here = state_ref[f]
    wide_ref[edge : edge + rows] = here
    after_ref[...] = wide_ref[edge + 1 : edge + 1 + rows]
    before_ref[...] = wide_ref[edge - 1 : edge - 1 + rows]
    after_ref[pl.ds(per_layer - 1, layers, stride=per_layer)] = strips_ref[f, :layers]
    before_ref[pl.ds(0, layers, stride=per_layer)] = strips_ref[f, layers:]
    after = after_ref[...]
    before = before_ref[...]
    sums = []
    for k in range(1, GHOST + 1):
        low = edge - k * per_layer
        high = edge + k * per_layer
        total = wide_ref[low : low + rows] + wide_ref[high : high + rows]
        step = DEPTH * k
        total += pltpu.roll(jnp.where(lane >= step, here, after), LANES - step, 1)
        total += pltpu.roll(jnp.where(lane < LANES - step, here, before), step, 1)
        total += pltpu.roll(jnp.where(depth >= k, here, 0.0), LANES - k, 1)
        total += pltpu.roll(jnp.where(depth < DEPTH - k, here, 0.0), k, 1)
        sums.append(total)
    return here, sums


def pair_rates(here, curvature, metric_sums, curvature_sums, half, pull):
    one, two, three = metric_sums
    damping = (three - 6.0 * two + 15.0 * one - 60.0 * here) * DAMP
    laplace = (16.0 * one - two - 90.0 * here) * LAPL
    metric_rate = 4.0 * half * curvature + damping
    one, two, three = curvature_sums
    damping = (three - 6.0 * two + 15.0 * one - 60.0 * curvature) * DAMP
    return metric_rate, half * laplace + pull * curvature + damping


def early_kernel(
    per_layer, count, state_ref, strips_ref, base_ref, accum_ref, next_ref, total_ref, half_ref, pull_ref,
    wide_ref, after_ref, before_ref,
):
    fields, rows, _ = state_ref.shape
    halves = fields // 2
    edge = GHOST * per_layer
    lane = lane_index(rows)
    lapse = 1.0 + 0.25 * jnp.tanh(state_ref[0])
    trace = state_ref[halves]
    for f in range(halves + 1, fields):
        trace = trace + state_ref[f]
    half_ref[...] = -0.5 * lapse
    pull_ref[...] = lapse * trace * (1.0 / halves)
    wide_ref[:edge] = jnp.zeros((edge, LANES), jnp.float32)
    wide_ref[edge + rows :] = jnp.zeros((edge, LANES), jnp.float32)

    def body(f, carry):
        sums = lambda at: field_sums(per_layer, lane, state_ref, strips_ref, at, wide_ref, after_ref, before_ref)
        u, u_sums = sums(f)
        v, v_sums = sums(f + halves)
        rates = pair_rates(u, v, u_sums, v_sums, half_ref[...], pull_ref[...])
        for at, rate in zip((f, f + halves), rates):
            next_ref[at] = base_ref[at] + (SECTION_SHIFT * TIME_STEP) * rate
            total_ref[at] = accum_ref[at] + (SECTION_WEIGHT * TIME_STEP) * rate
        return carry

    lax.fori_loop(0, count, body, 0)


def late_kernel(
    per_layer, count, state_ref, layers_ref, strips_ref, base_ref, accum_ref, half_ref, pull_ref, next_in, total_in,
    next_ref, total_ref, wide_ref, after_ref, before_ref, low_ref, high_ref,
):
    fields, rows, _ = state_ref.shape
    halves = fields // 2
    edge = GHOST * per_layer
    reach = -(-edge // 8) * 8
    lane = lane_index(rows)
    low_ref[edge:] = jnp.zeros((reach, LANES), jnp.float32)
    high_ref[:reach] = jnp.zeros((reach, LANES), jnp.float32)

    def ends(f):
        low_ref[:edge] = layers_ref[f, edge:]
        high_ref[reach:] = layers_ref[f, :edge]
        out = []
        for buf, at in ((low_ref, lambda k: edge - k * per_layer), (high_ref, lambda k: k * per_layer)):
            one, two, three = (buf[at(k) : at(k) + reach] for k in (1, 2, 3))
            out.append(((three - 6.0 * two + 15.0 * one) * DAMP, (16.0 * one - two) * LAPL))
        return out

    def mend(f, carry):
        for at, u, v in zip((slice(0, reach), slice(rows - reach, rows)), ends(f), ends(f + halves)):
            for field, rate in ((f, u[0]), (f + halves, v[0] + half_ref[at] * u[1])):
                next_ref[field, at] = next_in[field, at] + (SECTION_SHIFT * TIME_STEP) * rate
                total_ref[field, at] = total_in[field, at] + (SECTION_WEIGHT * TIME_STEP) * rate
        return carry

    lax.fori_loop(0, count, mend, 0)

    def body(f, carry):
        def sums(at):
            wide_ref[:edge] = layers_ref[at, edge:]
            wide_ref[edge + rows :] = layers_ref[at, :edge]
            return field_sums(per_layer, lane, state_ref, strips_ref, at, wide_ref, after_ref, before_ref)

        u, u_sums = sums(f)
        v, v_sums = sums(f + halves)
        rates = pair_rates(u, v, u_sums, v_sums, half_ref[...], pull_ref[...])
        for at, rate in zip((f, f + halves), rates):
            next_ref[at] = base_ref[at] + (SECTION_SHIFT * TIME_STEP) * rate
            total_ref[at] = accum_ref[at] + (SECTION_WEIGHT * TIME_STEP) * rate
        return carry

    lax.fori_loop(count, halves, body, 0)


def final_kernel(columns, owner_ref, me_ref, half_ref, next_ref, total_ref, *refs):
    count = len(refs) - 6
    sources = refs[:count]
    next_out, total_out, lapl_ref, next_buf, total_buf, sems = refs[count:]
    fields, rows, _ = next_ref.shape
    halves = fields // 2
    groups = sources[0].shape[0]
    me = me_ref[0]
    below, above = neighbours(owner_ref, me, columns)
    low_from = me ^ below
    high_from = me ^ above
    one_lane = lane_index(8)
    depth = one_lane % DEPTH
    slot = (depth + DEPTH - SLOT) % DEPTH
    low_at = jnp.where(slot < SLOTS * SLOT, slot % SLOT, SLOT)
    high_at = jnp.where(depth < SLOTS * SLOT, depth % SLOT, 0)

    def widen(x):
        return jnp.concatenate([x] * (rows // 8), axis=0)

    def per_lane(position, values):
        out = jnp.zeros((8, LANES), jnp.float32)
        for at, value in values:
            out = jnp.where(position == at, value, out)
        return widen(out)

    low_damp = [
        per_lane(low_at, v)
        for v in (
            ((0, 1.0 * DAMP), (1, 1.0 * DAMP), (2, 1.0 * DAMP)),
            ((0, -6.0 * DAMP), (1, -6.0 * DAMP)),
            ((0, 15.0 * DAMP),),
        )
    ]
    high_damp = [
        per_lane(high_at, v)
        for v in (
            ((3, 1.0 * DAMP), (4, 1.0 * DAMP), (5, 1.0 * DAMP)),
            ((4, -6.0 * DAMP), (5, -6.0 * DAMP)),
            ((5, 15.0 * DAMP),),
        )
    ]
    low_lapl = [per_lane(low_at, v) for v in (((0, -LAPL), (1, -LAPL)), ((0, 16.0 * LAPL),))]
    high_lapl = [per_lane(high_at, v) for v in (((4, -LAPL), (5, -LAPL)), ((5, 16.0 * LAPL),))]
    low_masks = [jnp.full((rows, LANES), low_from) == d for d in range(1, count)]
    high_masks = [jnp.full((rows, LANES), high_from) == d for d in range(1, count)]
    at_edge = widen(((depth < GHOST) | (depth >= DEPTH - GHOST)).astype(jnp.float32)) > 0.5
    half = half_ref[...]
    shift = 2 * DEPTH + SLOT

    def spread(packed, f):
        moved = pltpu.roll(packed, (DEPTH - SLOT - SLOT * (f % SLOTS)) % LANES, 1)
        return jnp.where(at_edge, moved, 0.0)

    copies = []
    for g in range(groups):
        low = high = sources[0][g]
        for low_mask, high_mask, source in zip(low_masks, high_masks, sources[1:]):
            low = jnp.where(low_mask, source[g], low)
            high = jnp.where(high_mask, source[g], high)
        low_0 = pltpu.roll(low, shift, 1)
        low_1 = pltpu.roll(low, shift - 1, 1)
        low_2 = pltpu.roll(low, shift - 2, 1)
        high_1 = pltpu.roll(high, 1, 1)
        high_2 = pltpu.roll(high, 2, 1)
        damp = (
            low_damp[0] * low_0 + low_damp[1] * low_1 + low_damp[2] * low_2
            + high_damp[0] * high + high_damp[1] * high_1 + high_damp[2] * high_2
        )
        if g * SLOTS < halves:
            lapl_ref[g] = (
                low_lapl[0] * low_1 + low_lapl[1] * low_2
                + high_lapl[0] * high_1 + high_lapl[1] * high_2
            )
        first = g * SLOTS
        last = min(first + SLOTS, fields)
        for f in range(first, last):
            rate = spread(damp, f)
            if f >= halves:
                rate = rate + half * spread(lapl_ref[(f - halves) // SLOTS], f - halves)
            next_buf[f] = next_ref[f] + (SECTION_SHIFT * TIME_STEP) * rate
            total_buf[f] = total_ref[f] + (SECTION_WEIGHT * TIME_STEP) * rate
        part = pl.ds(first, last - first)
        for which, (buf, out) in enumerate(((next_buf, next_out), (total_buf, total_out))):
            copy = pltpu.make_async_copy(buf.at[part], out.at[part], sems.at[which, g])
            copy.start()
            copies.append(copy)
    for copy in copies:
        copy.wait()


def swap_ends(ends, axis):
    count = lax.axis_size(axis)
    if count == 2:
        return lax.ppermute(ends, axis, [(0, 1), (1, 0)])
    low, high = jnp.split(ends, 2, axis=1)
    forward = [(i, (i + 1) % count) for i in range(count)]
    backward = [(target, source) for source, target in forward]
    return jnp.concatenate([lax.ppermute(low, axis, backward), lax.ppermute(high, axis, forward)], axis=1)


def routed(packed, owner):
    columns = lax.axis_size("gz")
    labels = jnp.arange(columns, dtype=jnp.int32)
    matches = owner[:, None] == labels[None, :]
    column_of = jnp.sum(jnp.where(matches, labels[:, None], 0), axis=0)
    below = jnp.take(owner, (column_of + columns - 1) % columns)
    above = jnp.take(owner, (column_of + 1) % columns)
    groups, rows, _ = packed.shape
    pieces = packed.reshape(groups, columns, rows // columns, LANES).transpose(1, 0, 2, 3)
    spread = lax.all_to_all(pieces, "gz", split_axis=0, concat_axis=0, tiled=True)
    low_part = (jnp.arange(LANES) % DEPTH) % SLOT < GHOST
    forwarded = jnp.where(low_part, spread[below], spread[above])
    arrived = lax.all_to_all(forwarded, "gz", split_axis=0, concat_axis=0, tiled=True)
    return arrived.transpose(1, 0, 2, 3).reshape(groups, rows, LANES)


def substep(state, base, accum, owner):
    fields, thickness, _, cells = state.shape
    per_layer = cells // LANES
    rows = thickness * per_layer
    shape = (fields, rows, LANES)
    columns = lax.axis_size("gz")
    me = lax.axis_index("gz").reshape(1).astype(jnp.int32)
    cells_in = state.reshape(shape)
    base = base.reshape(shape)
    accum = accum.reshape(shape)
    groups = -(-fields // SLOTS)
    f32 = lambda *s: jax.ShapeDtypeStruct(s, jnp.float32)
    whole = fields * rows * LANES * 4
    smem = pl.BlockSpec(memory_space=SMEM)
    anywhere = pl.BlockSpec(memory_space=pl.ANY)

    packed = call(pack_faces_kernel, f32(groups, rows, LANES), [vmem_spec()], cost=(whole, whole))(cells_in)
    if direct(columns):
        near = columns // 2
        cross = columns // 2 + columns // 4
        got = []
        for d in range(1, near):
            got.append(exchange(packed, d))
        forwarded = call(
            functools.partial(forward_kernel, columns, cross), f32(groups, rows, LANES),
            [smem, smem] + [vmem_spec() for _ in range(near)], cost=(whole, whole),
        )(owner, me, packed, *got)
        candidates = [exchange(forwarded, cross)] + got
    else:
        candidates = [routed(packed, owner)]

    layers, strips = call(
        functools.partial(pack_ends_kernel, per_layer),
        [f32(fields, 2 * GHOST * per_layer, LANES), f32(fields, 2 * thickness, LANES)],
        [vmem_spec()], cost=(whole, whole),
    )(cells_in)
    layers = swap_ends(layers, "gx")
    strips = swap_ends(strips, "gy")
    edge = GHOST * per_layer
    count = fields // 4
    reach = -(-edge // 8) * 8
    rolls = [VMEM((rows + 2 * edge, LANES), jnp.float32), VMEM((rows, LANES), jnp.float32), VMEM((rows, LANES), jnp.float32)]
    part_next, part_total, half, pull = call(
        functools.partial(early_kernel, per_layer, count),
        [f32(*shape), f32(*shape), f32(rows, LANES), f32(rows, LANES)],
        [vmem_spec() for _ in range(4)],
        scratch=rolls, cost=(30 * whole, 3 * whole),
    )(cells_in, strips, base, accum)
    part_next, part_total = call(
        functools.partial(late_kernel, per_layer, count),
        [f32(*shape), f32(*shape)],
        [vmem_spec() for _ in range(9)],
        scratch=rolls + [VMEM((edge + reach, LANES), jnp.float32), VMEM((edge + reach, LANES), jnp.float32)],
        cost=(30 * whole, 3 * whole), aliases={7: 0, 8: 1},
    )(cells_in, layers, strips, base, accum, half, pull, part_next, part_total)
    next_section, accum_out = call(
        functools.partial(final_kernel, columns), [f32(*shape), f32(*shape)],
        [smem, smem] + [vmem_spec() for _ in range(3 + len(candidates))],
        out_specs=[anywhere, anywhere],
        scratch=[VMEM((-(-(fields // 2) // SLOTS), rows, LANES), jnp.float32)]
        + [VMEM(shape, jnp.float32) for _ in range(2)]
        + [pltpu.SemaphoreType.DMA((2, groups))],
        cost=(10 * whole, 4 * whole),
    )(owner, me, half, part_next, part_total, *candidates)
    return (next_section.reshape(state.shape), accum_out.reshape(state.shape))


def direct(columns):
    return 2 < columns <= 8 and columns & (columns - 1) == 0


def exchange(x, d):
    columns = lax.axis_size("gz")
    return lax.ppermute(x, "gz", [(i, i ^ d) for i in range(columns)])


def solution(mesh):
    step = jax.shard_map(
        substep,
        mesh=mesh,
        in_specs=(
            P(None, "gx", ("gy", "gz"), None),
            P(None, "gx", ("gy", "gz"), None),
            P(None, "gx", ("gy", "gz"), None),
            P(),
        ),
        out_specs=(P(None, "gx", ("gy", "gz"), None), P(None, "gx", ("gy", "gz"), None)),
        check_vma=False,
    )
    columns = mesh.shape["gz"]
    if not direct(columns):
        return step
    return step
```

profile of v0, /device:TPU:0, one launch (start us, length us, event | category | flops | bytes accessed | tf_op | source)
XLA Modules:
  0.0 27.4 jit_solution(18140743724451270329)
XLA Ops:
  0.6 0.0 copy-start
  0.6 1.1 %copy-done = f32[24,16,1,512]{3,2,1,0:T(1,128)S(1)} copy-done((f32[24,16,1,512]{3,2,1,0:T(1,128)S(1)}, f32[24,16,1,512]{3,2,1,0:T(1,128)}, u32[]{:S(2)}) %copy-start) | copy-done | bytes 786456
  1.8 0.0 copy-start.4
  1.8 0.0 copy-start.3
  1.8 0.9 %shard_map.59 = (f32[24,24,128]{2,1,0:T(8,128)}, f32[24,32,128]{2,1,0:T(8,128)}) custom-call(f32[24,64,128]{2,1,0:T(8,128)S(1)} %bitcast.6), custom_call_target="tpu_custom_call" | custom-call | flops 786432 | bytes 786432 | tf_op jit(solution)/shard_map/pallas_call | solution.py:371
  2.7 0.0 copy-start.1
  2.7 0.0 copy-start.2
  2.7 0.5 %collective-permute-start = (f32[24,32,128]{2,1,0:T(8,128)}, f32[24,32,128]{2,1,0:T(8,128)S(1)}, u32[]{:S(2)}, u32[]{:S(2)}) collective-permute-start(f32[24,32,128]{2,1,0:T(8,128)} %get-tuple-element.12), channel_id=1, source_target_pairs={{0,8},{8,0},{1,9},{9,1},{2,10},{10,2},{3,11},{11,3},{4,12},{12,4},... | collective-permute-start | bytes 1179656 | tf_op jit(solution)/shard_map/ppermute | solution.py:317
  3.2 0.3 shard_map.62.refs_0_
  3.4 2.6 %collective-permute-start.2 = (f32[5,64,128]{2,1,0:T(8,128)S(1)}, f32[5,64,128]{2,1,0:T(8,128)S(1)}, u32[]{:S(2)}, u32[]{:S(2)}) collective-permute-start(f32[5,64,128]{2,1,0:T(8,128)S(1)} %shard_map.62.refs_0_), channel_id=1, source_target_pairs={{0,1},{1,0},{2,3},{3,2},{4,5},{5,4},{6,7},{7,6},{8,9},{9,8},{10,11... | collective-permute-start | bytes 491528 | tf_op jit(solution)/shard_map/ppermute | solution.py:413
  6.0 1.6 %collective-permute-start.3 = (f32[5,64,128]{2,1,0:T(8,128)S(1)}, f32[5,64,128]{2,1,0:T(8,128)S(1)}, u32[]{:S(2)}, u32[]{:S(2)}) collective-permute-start(f32[5,64,128]{2,1,0:T(8,128)S(1)} %shard_map.62.refs_0_), channel_id=1, source_target_pairs={{0,2},{1,3},{2,0},{3,1},{4,6},{5,7},{6,4},{7,5},{8,10},{9,11},{10,... | collective-permute-start | bytes 491528 | tf_op jit(solution)/shard_map/ppermute | solution.py:413
  7.6 0.0 collective-permute-start.4
  7.6 1.9 %collective-permute-start.1 = (f32[24,24,128]{2,1,0:T(8,128)}, f32[24,24,128]{2,1,0:T(8,128)}, u32[]{:S(2)}, u32[]{:S(2)}) collective-permute-start(f32[24,24,128]{2,1,0:T(8,128)} %get-tuple-element.14), channel_id=1, source_target_pairs={{0,16},{16,0},{1,17},{17,1},{2,18},{18,2},{3,19},{19,3},{4,20},{20... | collective-permute-start | bytes 884744 | tf_op jit(solution)/shard_map/ppermute | solution.py:317
  9.5 1.4 %collective-permute-done.2.refs_1_ = f32[5,64,128]{2,1,0:T(8,128)S(1)} collective-permute-done((f32[5,64,128]{2,1,0:T(8,128)S(1)}, f32[5,64,128]{2,1,0:T(8,128)S(1)}, u32[]{:S(2)}, u32[]{:S(2)}) %collective-permute-start.2) | collective-permute-done | bytes 163872 | tf_op jit(solution)/shard_map/ppermute | solution.py:413
  10.9 2.2 %collective-permute-done.3.refs_2_ = f32[5,64,128]{2,1,0:T(8,128)S(1)} collective-permute-done((f32[5,64,128]{2,1,0:T(8,128)S(1)}, f32[5,64,128]{2,1,0:T(8,128)S(1)}, u32[]{:S(2)}, u32[]{:S(2)}) %collective-permute-start.3) | collective-permute-done | bytes 163872 | tf_op jit(solution)/shard_map/ppermute | solution.py:413
  13.1 2.6 %collective-permute-done.4.refs_3_ = f32[5,64,128]{2,1,0:T(8,128)S(1)} collective-permute-done((f32[5,64,128]{2,1,0:T(8,128)S(1)}, f32[5,64,128]{2,1,0:T(8,128)S(1)}, u32[]{:S(2)}, u32[]{:S(2)}) %collective-permute-start.4) | collective-permute-done | bytes 163872 | tf_op jit(solution)/shard_map/ppermute | solution.py:413
  15.6 0.0 copy-done.4
  15.6 0.7 %shard_map.63 = f32[5,64,128]{2,1,0:T(8,128)S(1)} custom-call(s32[8]{0:T(128)S(1)} %copy-done.4, s32[1]{0:T(128)} %bitcast.me_ref, f32[5,64,128]{2,1,0:T(8,128)S(1)} %shard_map.62.refs_0_, f32[5,64,128]{2,1,0:T(8,128)S(1)} %collective-permute-done.2.refs_1_, f32[5,64,128]{2,1,0:T(8,128)S(1)} %collective-permute-done.3.refs_2_, ...), custom_call_target="tpu_custom_call" | custom-call | flops 786432 | bytes 786432 | tf_op jit(solution)/shard_map/pallas_call | solution.py:363
  16.3 3.8 %collective-permute-start.5 = (f32[5,64,128]{2,1,0:T(8,128)S(1)}, f32[5,64,128]{2,1,0:T(8,128)S(1)}, u32[]{:S(2)}, u32[]{:S(2)}) collective-permute-start(f32[5,64,128]{2,1,0:T(8,128)S(1)} %shard_map.63), channel_id=1, source_target_pairs={{0,6},{1,7},{2,4},{3,5},{4,2},{5,3},{6,0},{7,1},{8,14},{9,15},{10,... | collective-permute-start | bytes 491528 | tf_op jit(solution)/shard_map/ppermute | solution.py:413
  20.1 0.0 collective-permute-done.strips_ref
  20.1 0.0 copy-done.3
  20.1 0.0 copy-done.1
  20.1 0.0 copy-done.2
  20.1 1.9 %shard_map.60 = (f32[24,64,128]{2,1,0:T(8,128)S(1)}, f32[24,64,128]{2,1,0:T(8,128)S(1)}, f32[64,128]{1,0:T(8,128)S(1)}, f32[64,128]{1,0:T(8,128)S(1)}) custom-call(f32[24,64,128]{2,1,0:T(8,128)S(1)} %bitcast.8, f32[24,32,128]{2,1,0:T(8,128)S(1)} %collective-permute-done.strips_ref, f32[24,64,128]{2,1,0:T(8,128)S(1)} %bitcast.10, f32[24,64,128]{2,1,0:T(8,128)S(1)} %bitcast.12), custom_call_target="tpu_custom_call" | custom-call | flops 23592960 | bytes 2359296 | tf_op jit(solution)/shard_map/pallas_call | solution.py:382
  22.0 0.0 collective-permute-done.1.layers_ref
  22.0 3.0 %shard_map.61 = (f32[24,64,128]{2,1,0:T(8,128)S(1)}, f32[24,64,128]{2,1,0:T(8,128)S(1)}) custom-call(f32[24,64,128]{2,1,0:T(8,128)S(1)} %bitcast.9, f32[24,24,128]{2,1,0:T(8,128)} %collective-permute-done.1.layers_ref, f32[24,32,128]{2,1,0:T(8,128)S(1)} %collective-permute-done.strips_ref, ...), custom_call_target="tpu_custom_call", output_to_operand_aliasing={{0}: (7, {}), {1}: (8, {})} | custom-call | flops 23592960 | bytes 2359296 | tf_op jit(solution)/shard_map/pallas_call | solution.py:388
  25.0 0.0 collective-permute-done.5.refs_0_
  25.0 2.3 %shard_map.64 = (f32[24,64,128]{2,1,0:T(8,128)}, f32[24,64,128]{2,1,0:T(8,128)}) custom-call(s32[8]{0:T(128)S(1)} %copy-done.4, s32[1]{0:T(128)} %bitcast.me_ref, f32[64,128]{1,0:T(8,128)S(1)} %get-tuple-element.13.half_ref, f32[24,64,128]{2,1,0:T(8,128)S(1)} %get-tuple-element.18.next_ref, f32[24,64,128]{2,1,0:T(8,128)S(1)} %get-tuple-element.19.total_ref, ...), custom_call_target="tpu_custom_call" | custom-call | flops 7864320 | bytes 3145728 | tf_op jit(solution)/shard_map/pallas_call | solution.py:395
Async XLA Ops:
  0.6 1.1 %copy-start = (f32[24,16,1,512]{3,2,1,0:T(1,128)S(1)}, f32[24,16,1,512]{3,2,1,0:T(1,128)}, u32[]{:S(2)}) copy-start(f32[24,16,1,512]{3,2,1,0:T(1,128)} %param.4) | copy-start | bytes 2359300
  1.8 13.9 %copy-start.4 = (s32[8]{0:T(128)S(1)}, s32[8]{0:T(128)}, u32[]{:S(2)}) copy-start(s32[8]{0:T(128)} %owner_ref.3) | copy-start | bytes 100
  1.8 18.4 %copy-start.3 = (f32[24,16,1,512]{3,2,1,0:T(1,128)S(1)}, f32[24,16,1,512]{3,2,1,0:T(1,128)}, u32[]{:S(2)}) copy-start(f32[24,16,1,512]{3,2,1,0:T(1,128)} %param.6) | copy-start | bytes 2359300
  2.7 17.5 %copy-start.1 = (f32[24,16,1,512]{3,2,1,0:T(1,128)S(1)}, f32[24,16,1,512]{3,2,1,0:T(1,128)}, u32[]{:S(2)}) copy-start(f32[24,16,1,512]{3,2,1,0:T(1,128)} %param.4) | copy-start | bytes 2359300
  2.7 17.5 %copy-start.2 = (f32[24,16,1,512]{3,2,1,0:T(1,128)S(1)}, f32[24,16,1,512]{3,2,1,0:T(1,128)}, u32[]{:S(2)}) copy-start(f32[24,16,1,512]{3,2,1,0:T(1,128)} %param.5) | copy-start | bytes 2359300
  2.7 17.5 %collective-permute-start = (f32[24,32,128]{2,1,0:T(8,128)}, f32[24,32,128]{2,1,0:T(8,128)S(1)}, u32[]{:S(2)}, u32[]{:S(2)}) collective-permute-start(f32[24,32,128]{2,1,0:T(8,128)} %get-tuple-element.12), channel_id=1, source_target_pairs={{0,8},{8,0},{1,9},{9,1},{2,10},{10,2},{3,11},{11,3},{4,12},{12,4},... | collective-permute-start | bytes 1179656 | tf_op jit(solution)/shard_map/ppermute | solution.py:317
  3.4 7.4 %collective-permute-start.2 = (f32[5,64,128]{2,1,0:T(8,128)S(1)}, f32[5,64,128]{2,1,0:T(8,128)S(1)}, u32[]{:S(2)}, u32[]{:S(2)}) collective-permute-start(f32[5,64,128]{2,1,0:T(8,128)S(1)} %shard_map.62.refs_0_), channel_id=1, source_target_pairs={{0,1},{1,0},{2,3},{3,2},{4,5},{5,4},{6,7},{7,6},{8,9},{9,8},{10,11... | collective-permute-start | bytes 491528 | tf_op jit(solution)/shard_map/ppermute | solution.py:413
  6.0 7.1 %collective-permute-start.3 = (f32[5,64,128]{2,1,0:T(8,128)S(1)}, f32[5,64,128]{2,1,0:T(8,128)S(1)}, u32[]{:S(2)}, u32[]{:S(2)}) collective-permute-start(f32[5,64,128]{2,1,0:T(8,128)S(1)} %shard_map.62.refs_0_), channel_id=1, source_target_pairs={{0,2},{1,3},{2,0},{3,1},{4,6},{5,7},{6,4},{7,5},{8,10},{9,11},{10,... | collective-permute-start | bytes 491528 | tf_op jit(solution)/shard_map/ppermute | solution.py:413
  7.6 8.1 %collective-permute-start.4 = (f32[5,64,128]{2,1,0:T(8,128)S(1)}, f32[5,64,128]{2,1,0:T(8,128)S(1)}, u32[]{:S(2)}, u32[]{:S(2)}) collective-permute-start(f32[5,64,128]{2,1,0:T(8,128)S(1)} %shard_map.62.refs_0_), channel_id=1, source_target_pairs={{0,3},{1,2},{2,1},{3,0},{4,7},{5,6},{6,5},{7,4},{8,11},{9,10},{10,... | collective-permute-start | bytes 491528 | tf_op jit(solution)/shard_map/ppermute | solution.py:413
  7.6 14.4 %collective-permute-start.1 = (f32[24,24,128]{2,1,0:T(8,128)}, f32[24,24,128]{2,1,0:T(8,128)}, u32[]{:S(2)}, u32[]{:S(2)}) collective-permute-start(f32[24,24,128]{2,1,0:T(8,128)} %get-tuple-element.14), channel_id=1, source_target_pairs={{0,16},{16,0},{1,17},{17,1},{2,18},{18,2},{3,19},{19,3},{4,20},{20... | collective-permute-start | bytes 884744 | tf_op jit(solution)/shard_map/ppermute | solution.py:317
  16.3 8.7 %collective-permute-start.5 = (f32[5,64,128]{2,1,0:T(8,128)S(1)}, f32[5,64,128]{2,1,0:T(8,128)S(1)}, u32[]{:S(2)}, u32[]{:S(2)}) collective-permute-start(f32[5,64,128]{2,1,0:T(8,128)S(1)} %shard_map.63), channel_id=1, source_target_pairs={{0,6},{1,7},{2,4},{3,5},{4,2},{5,3},{6,0},{7,1},{8,14},{9,15},{10,... | collective-permute-start | bytes 491528 | tf_op jit(solution)/shard_map/ppermute | solution.py:413
where the time goes:
time: 27.5 us; the launch traced here: 27.4 us
  starting transfers between devices  10.3 us (37%)
  Pallas kernels  8.98 us (33%)
  waiting for transfers between devices  6.18 us (22%)
  local copies, waits for them, and re-layouts  1.14 us (4%)
  between operations  0.71 us (3%)
    ppermute x4, starting transfers between devices, exchange(): return lax.ppermute(x, 'gz', [(i, i ^ d) for i in range(columns)])  7.96 us
    ppermute x4, waiting for transfers between devices, exchange(): return lax.ppermute(x, 'gz', [(i, i ^ d) for i in range(columns)])  6.18 us
    pallas_call x1, Pallas kernels, substep(): call(functools.partial(late_kernel, per_layer, count), [f32(*shape), f32(...  2.98 us
    ppermute x2, starting transfers between devices, swap_ends(): return lax.ppermute(ends, axis, [(0, 1), (1, 0)])  2.37 us
    pallas_call x1, Pallas kernels, substep(): call(functools.partial(final_kernel, columns), [f32(*shape), f32(*shape)]...  2.32 us
    pallas_call x1, Pallas kernels, substep(): call(functools.partial(early_kernel, per_layer, count), [f32(*shape), f32...  1.87 us
    unnamed x10, local copies, waits for them, and re-layouts  1.14 us
    pallas_call x1, Pallas kernels, substep(): call(functools.partial(pack_ends_kernel, per_layer), [f32(fields, 2 * GHO...  0.9 us
  transfers between devices with their start and end apart: 6, of which 3 were waited for; matrix products, arithmetic and copies ran while one was open for 0% of the time, Pallas kernels for 21%

commit v1 on v0

v1 whole, which is shorter than its diff:
```python
import functools
import math

import jax
import jax.numpy as jnp
from jax import lax
from jax.experimental import pallas as pl
from jax.experimental.pallas import tpu as pltpu
from jax.sharding import PartitionSpec as P


BLOCK = 16


DAMPING_STRENGTH = 1.0
SPACING = 1.0
TIME_STEP = 0.25
SECTION_SHIFT = 0.5
SECTION_WEIGHT = 1.0 / 3.0

LANES = 128
TILE = 8
LIMIT = 16 * 2**20
GHOST = 3
SLOT = 2 * GHOST
DEPTH = 2 * BLOCK
ARRAYS = math.lcm(DEPTH, SLOT) // DEPTH
SLOTS = ARRAYS * DEPTH // SLOT
DAMP = DAMPING_STRENGTH / (64.0 * SPACING)
LAPL = 1.0 / (12.0 * SPACING * SPACING)
VMEM = pltpu.VMEM
SMEM = pltpu.SMEM


def vmem_spec():
    return pl.BlockSpec(memory_space=VMEM)


def call(kernel, outs, in_specs, out_specs=None, scratch=(), cost=None):
    multiple = isinstance(outs, (list, tuple))
    if out_specs is None:
        out_specs = [vmem_spec() for _ in outs] if multiple else vmem_spec()
    return pl.pallas_call(
        kernel,
        out_shape=outs,
        in_specs=in_specs,
        out_specs=out_specs,
        scratch_shapes=list(scratch),
        compiler_params=pltpu.CompilerParams(vmem_limit_bytes=LIMIT),
        cost_estimate=pl.CostEstimate(flops=cost[0], bytes_accessed=cost[1], transcendentals=0),
    )


def lane_index(rows):
    return lax.broadcasted_iota(jnp.int32, (rows, LANES), 1)


def blocks(fields):
    whole = fields - fields % SLOTS
    out = [[(first + k, half) for k in range(SLOTS)] for first in range(0, whole, SLOTS) for half in (0, 1)]
    rest = range(whole, fields)
    assert len(rest) in (0, SLOTS // 2)
    return out + ([[(f, half) for half in (0, 1) for f in rest]] if rest else [])


def half_rows(half, rows):
    return slice(half * rows, (half + 1) * rows)


def plane(array, lane):
    return array * DEPTH + lane % DEPTH


def pack_faces_kernel(state_ref, out_ref):
    rows = out_ref.shape[2]
    lane = lane_index(rows)
    for at, block in enumerate(blocks(state_ref.shape[0])):
        moved = [
            pltpu.roll(state_ref[f, half_rows(half, rows)], (GHOST + SLOT * k) % LANES, 1)
            for k, (f, half) in enumerate(block)
        ]
        for array in range(ARRAYS):
            slot = plane(array, lane) // SLOT
            first = array * DEPTH // SLOT
            packed = moved[first]
            for k in range(first + 1, (array * DEPTH + DEPTH - 1) // SLOT + 1):
                packed = jnp.where(slot == k, moved[k], packed)
            out_ref[at, array] = packed


def pack_ends_kernel(per_layer, state_ref, layers_ref, strips_ref):
    fields, rows, _ = state_ref.shape
    edge = GHOST * per_layer
    layers = rows // per_layer
    layers_ref[:, :edge] = state_ref[:, :edge]
    layers_ref[:, edge:] = state_ref[:, rows - edge :]
    for f in range(fields):
        strips_ref[f, :layers] = state_ref[f, pl.ds(0, layers, stride=per_layer)]
        strips_ref[f, layers:] = state_ref[f, pl.ds(per_layer - 1, layers, stride=per_layer)]


def find_column(owner_ref, device, columns):
    def body(t, found):
        return jnp.where(owner_ref[t] == device, t, found)

    return lax.fori_loop(0, columns, body, jnp.int32(0))


def neighbours(owner_ref, device, columns):
    column = find_column(owner_ref, device, columns)
    below = owner_ref[lax.rem(column + columns - 1, columns)]
    above = owner_ref[lax.rem(column + 1, columns)]
    return below, above


def routes_kernel(columns, cross, owner_ref, me_ref, out_ref):
    me = me_ref[0]
    below, above = neighbours(owner_ref, me, columns)
    there, beyond = neighbours(owner_ref, me ^ cross, columns)
    shape = out_ref.shape[1:]
    for array in range(ARRAYS):
        low_part = plane(array, lane_index(shape[0])) % SLOT < GHOST
        out_ref[array] = jnp.where(low_part, me ^ there, me ^ beyond)
    out_ref[ARRAYS] = jnp.full(shape, me ^ below, jnp.int32)
    out_ref[ARRAYS + 1] = jnp.full(shape, me ^ above, jnp.int32)


def tiles(rows):
    return [slice(start, start + TILE) for start in range(0, rows, TILE)]


def forward_kernel(routes_ref, *refs):
    *sources, out_ref = refs
    count, arrays, rows, _ = out_ref.shape
    for array in range(arrays):
        masks = [routes_ref[array] == d for d in range(1, len(sources))]
        for block in range(count):
            for at in tiles(rows):
                chosen = sources[0][block, array, at]
                for mask, source in zip(masks, sources[1:]):
                    chosen = jnp.where(mask, source[block, array, at], chosen)
                out_ref[block, array, at] = chosen


def field_sums(per_layer, lane, state_ref, strips_ref, f, wide_ref, after_ref, before_ref):
    rows = state_ref.shape[1]
    edge = GHOST * per_layer
    layers = rows // per_layer
    depth = lane % DEPTH
    here = state_ref[f]
    wide_ref[edge : edge + rows] = here
    after_ref[...] = wide_ref[edge + 1 : edge + 1 + rows]
    before_ref[...] = wide_ref[edge - 1 : edge - 1 + rows]
    after_ref[pl.ds(per_layer - 1, layers, stride=per_layer)] = strips_ref[f, :layers]
    before_ref[pl.ds(0, layers, stride=per_layer)] = strips_ref[f, layers:]
    after = after_ref[...]
    before = before_ref[...]
    sums = []
    for k in range(1, GHOST + 1):
        low = edge - k * per_layer
        high = edge + k * per_layer
        total = wide_ref[low : low + rows] + wide_ref[high : high + rows]
        step = DEPTH * k
        total += pltpu.roll(jnp.where(lane >= step, here, after), LANES - step, 1)
        total += pltpu.roll(jnp.where(lane < LANES - step, here, before), step, 1)
        total += pltpu.roll(jnp.where(depth >= k, here, 0.0), LANES - k, 1)
        total += pltpu.roll(jnp.where(depth < DEPTH - k, here, 0.0), k, 1)
        sums.append(total)
    return here, sums


def pair_rates(here, curvature, metric_sums, curvature_sums, half, pull):
    one, two, three = metric_sums
    damping = (three - 6.0 * two + 15.0 * one - 60.0 * here) * DAMP
    laplace = (16.0 * one - two - 90.0 * here) * LAPL
    metric_rate = 4.0 * half * curvature + damping
    one, two, three = curvature_sums
    damping = (three - 6.0 * two + 15.0 * one - 60.0 * curvature) * DAMP
    return metric_rate, half * laplace + pull * curvature + damping


def early_kernel(per_layer, count, state_ref, strips_ref, rates_ref, half_ref, pull_ref, wide_ref, after_ref, before_ref):
    fields, rows, _ = state_ref.shape
    halves = fields // 2
    edge = GHOST * per_layer
    lane = lane_index(rows)
    lapse = 1.0 + 0.25 * jnp.tanh(state_ref[0])
    trace = state_ref[halves]
    for f in range(halves + 1, fields):
        trace = trace + state_ref[f]
    half_ref[...] = -0.5 * lapse
    pull_ref[...] = lapse * trace * (1.0 / halves)
    wide_ref[:edge] = jnp.zeros((edge, LANES), jnp.float32)
    wide_ref[edge + rows :] = jnp.zeros((edge, LANES), jnp.float32)

    def body(f, carry):
        sums = lambda at: field_sums(per_layer, lane, state_ref, strips_ref, at, wide_ref, after_ref, before_ref)
        u, u_sums = sums(f)
        v, v_sums = sums(f + halves)
        rates_ref[f], rates_ref[f + count] = pair_rates(u, v, u_sums, v_sums, half_ref[...], pull_ref[...])
        return carry

    lax.fori_loop(0, count, body, 0)


def late_kernel(
    per_layer, count, state_ref, layers_ref, strips_ref, base_ref, accum_ref, half_ref, pull_ref, rates_ref,
    next_ref, total_ref, wide_ref, after_ref, before_ref, low_ref, high_ref,
):
    fields, rows, _ = state_ref.shape
    halves = fields // 2
    edge = GHOST * per_layer
    reach = -(-edge // TILE) * TILE
    lane = lane_index(rows)
    low_ref[edge:] = jnp.zeros((reach, LANES), jnp.float32)
    high_ref[:reach] = jnp.zeros((reach, LANES), jnp.float32)

    def write(f, at, rate):
        next_ref[f, at] = base_ref[f, at] + (SECTION_SHIFT * TIME_STEP) * rate
        total_ref[f, at] = accum_ref[f, at] + (SECTION_WEIGHT * TIME_STEP) * rate

    def ends(f):
        low_ref[:edge] = layers_ref[f, edge:]
        high_ref[reach:] = layers_ref[f, :edge]
        out = []
        for buf, at in ((low_ref, lambda k: edge - k * per_layer), (high_ref, lambda k: k * per_layer)):
            one, two, three = (buf[at(k) : at(k) + reach] for k in (1, 2, 3))
            out.append(((three - 6.0 * two + 15.0 * one) * DAMP, (16.0 * one - two) * LAPL))
        return out

    def mend(f, carry):
        for at, u, v in zip((slice(0, reach), slice(rows - reach, rows)), ends(f), ends(f + halves)):
            write(f, at, rates_ref[f, at] + u[0])
            write(f + halves, at, rates_ref[f + count, at] + v[0] + half_ref[at] * u[1])
        inner = slice(reach, rows - reach)
        write(f, inner, rates_ref[f, inner])
        write(f + halves, inner, rates_ref[f + count, inner])
        return carry

    lax.fori_loop(0, count, mend, 0)

    def body(f, carry):
        def sums(at):
            wide_ref[:edge] = layers_ref[at, edge:]
            wide_ref[edge + rows :] = layers_ref[at, :edge]
            return field_sums(per_layer, lane, state_ref, strips_ref, at, wide_ref, after_ref, before_ref)

        u, u_sums = sums(f)
        v, v_sums = sums(f + halves)
        rates = pair_rates(u, v, u_sums, v_sums, half_ref[...], pull_ref[...])
        write(f, slice(None), rates[0])
        write(f + halves, slice(None), rates[1])
        return carry

    lax.fori_loop(count, halves, body, 0)


def final_kernel(routes_ref, half_ref, next_ref, total_ref, *refs):
    count = len(refs) - 6
    sources = refs[:count]
    next_out, total_out, lapl_ref, next_buf, total_buf, sems = refs[count:]
    fields = next_ref.shape[0]
    halves = fields // 2
    rows = sources[0].shape[2]
    lane = lane_index(rows)
    depth = lane % DEPTH
    at_edge = (depth < GHOST) | (depth >= DEPTH - GHOST)
    low_masks, high_masks = (
        [jnp.concatenate([routes_ref[ARRAYS + side]] * (rows // TILE), axis=0) == d for d in range(1, count)]
        for side in (0, 1)
    )

    def chosen(block, array, masks):
        out = sources[0][block, array]
        for mask, source in zip(masks, sources[1:]):
            out = jnp.where(mask, source[block, array], out)
        return out

    def edge_rates(block):
        low = [chosen(block, array, low_masks) for array in range(ARRAYS)]
        high = [chosen(block, array, high_masks) for array in range(ARRAYS)]
        back = LANES - 2 * DEPTH + SLOT
        low = [[pltpu.roll(x, back - i, 1) for x in low] for i in range(GHOST)]
        high = [high] + [[pltpu.roll(x, i, 1) for x in high] for i in range(1, GHOST)]
        damping, laplace = [], []
        for array in range(ARRAYS):
            s = plane(array, lane) % SLOT
            is_low = s < GHOST
            near = [
                jnp.where(
                    is_low,
                    jnp.where(depth < SLOT - i, low[i][array - 1], low[i][array]),
                    jnp.where(depth < i, high[i][array - 1], high[i][array]) if i else high[0][array],
                )
                for i in range(GHOST)
            ]
            inner = (s == GHOST - 1) | (s == GHOST)
            outer = (s == 0) | (s == SLOT - 1)
            one = jnp.where(inner, 0.0, near[1])
            two = jnp.where(outer, near[2], 0.0)
            damping.append((near[0] - 6.0 * one + 15.0 * two) * DAMP)
            laplace.append((16.0 * two - one) * LAPL)
        return damping, laplace

    def spread(planes, k):
        first = (SLOT * k + GHOST) // DEPTH
        last = (SLOT * (k + 1) + GHOST - 1) // DEPTH % ARRAYS
        value = planes(first)
        if last != first:
            value = jnp.where(depth < DEPTH // 2, planes(last), value)
        return jnp.where(at_edge, pltpu.roll(value, (DEPTH - SLOT - SLOT * k) % LANES, 1), 0.0)

    layout = blocks(fields)
    place = {pair: (at, k) for at, block in enumerate(layout) for k, pair in enumerate(block)}
    copies = []
    for at, block in enumerate(layout):
        damping, laplace = edge_rates(at)
        if any(f < halves for f, _ in block):
            for array in range(ARRAYS):
                lapl_ref[at, array] = laplace[array]
        for part in range(2):
            piece = block[part * SLOTS // 2 : (part + 1) * SLOTS // 2]
            for k, (f, half) in enumerate(piece, part * SLOTS // 2):
                here = half_rows(half, rows)
                rate = spread(lambda array: damping[array], k)
                if f >= halves:
                    source, slot = place[(f - halves, half)]
                    rate = rate + half_ref[here] * spread(lambda array: lapl_ref[source, array], slot)
                next_buf[f, here] = next_ref[f, here] + (SECTION_SHIFT * TIME_STEP) * rate
                total_buf[f, here] = total_ref[f, here] + (SECTION_WEIGHT * TIME_STEP) * rate
            (first, half), (last, _) = piece[0], piece[-1]
            box = (pl.ds(first, last + 1 - first), pl.ds(half * rows, rows))
            for which, (buf, out) in enumerate(((next_buf, next_out), (total_buf, total_out))):
                copy = pltpu.make_async_copy(buf.at[box], out.at[box], sems.at[which, 2 * at + part])
                copy.start()
                copies.append(copy)
    for copy in copies:
        copy.wait()


def swap_ends(ends, axis):
    count = lax.axis_size(axis)
    if count == 2:
        return lax.ppermute(ends, axis, [(0, 1), (1, 0)])
    low, high = jnp.split(ends, 2, axis=1)
    forward = [(i, (i + 1) % count) for i in range(count)]
    backward = [(target, source) for source, target in forward]
    return jnp.concatenate([lax.ppermute(low, axis, backward), lax.ppermute(high, axis, forward)], axis=1)


def routed(packed, owner):
    columns = lax.axis_size("gz")
    labels = jnp.arange(columns, dtype=jnp.int32)
    matches = owner[:, None] == labels[None, :]
    column_of = jnp.sum(jnp.where(matches, labels[:, None], 0), axis=0)
    below = jnp.take(owner, (column_of + columns - 1) % columns)
    above = jnp.take(owner, (column_of + 1) % columns)
    total = math.prod(packed.shape[:-1])
    piece = -(-total // columns)
    pieces = lambda x: jnp.pad(x.reshape(total, LANES), ((0, piece * columns - total), (0, 0))).reshape(columns, piece, LANES)
    planes = jnp.arange(ARRAYS)[:, None] * DEPTH + jnp.arange(LANES) % DEPTH
    low_part = jnp.broadcast_to((planes % SLOT < GHOST)[None, :, None, :], packed.shape)
    low_part = pieces(low_part)[lax.axis_index("gz")]
    spread = lax.all_to_all(pieces(packed), "gz", split_axis=0, concat_axis=0, tiled=True)
    forwarded = jnp.where(low_part, spread[below], spread[above])
    arrived = lax.all_to_all(forwarded, "gz", split_axis=0, concat_axis=0, tiled=True)
    return arrived.reshape(piece * columns, LANES)[:total].reshape(packed.shape)


def substep(state, base, accum, owner):
    fields, thickness, _, cells = state.shape
    per_layer = cells // LANES
    rows = thickness * per_layer
    shape = (fields, rows, LANES)
    columns = lax.axis_size("gz")
    me = lax.axis_index("gz").reshape(1).astype(jnp.int32)
    cells_in = state.reshape(shape)
    base = base.reshape(shape)
    accum = accum.reshape(shape)
    faces = (len(blocks(fields)), ARRAYS, rows // 2, LANES)
    f32 = lambda *s: jax.ShapeDtypeStruct(s, jnp.float32)
    whole = fields * rows * LANES * 4
    smem = pl.BlockSpec(memory_space=SMEM)
    anywhere = pl.BlockSpec(memory_space=pl.ANY)

    packed = call(pack_faces_kernel, f32(*faces), [vmem_spec()], cost=(whole, whole))(cells_in)
    cross = columns // 2 + columns // 4 if direct(columns) else 0
    routes = call(
        functools.partial(routes_kernel, columns, cross),
        jax.ShapeDtypeStruct((ARRAYS + 2, TILE, LANES), jnp.int32), [smem, smem], cost=(whole // 4, whole // 4),
    )(owner, me)
    if direct(columns):
        near = columns // 2
        got = []
        for d in range(1, near):
            got.append(exchange(packed, d))
        forwarded = call(
            forward_kernel, f32(*faces),
            [vmem_spec() for _ in range(near + 1)], cost=(whole, whole),
        )(routes, packed, *got)
        candidates = [exchange(forwarded, cross)] + got
    else:
        candidates = [routed(packed, owner)]

    layers, strips = call(
        functools.partial(pack_ends_kernel, per_layer),
        [f32(fields, 2 * GHOST * per_layer, LANES), f32(fields, 2 * thickness, LANES)],
        [vmem_spec()], cost=(whole, whole),
    )(cells_in)
    layers = swap_ends(layers, "gx")
    strips = swap_ends(strips, "gy")
    edge = GHOST * per_layer
    count = fields // 4
    reach = -(-edge // TILE) * TILE
    rolls = [VMEM((rows + 2 * edge, LANES), jnp.float32), VMEM((rows, LANES), jnp.float32), VMEM((rows, LANES), jnp.float32)]
    rates, half, pull = call(
        functools.partial(early_kernel, per_layer, count),
        [f32(2 * count, rows, LANES), f32(rows, LANES), f32(rows, LANES)],
        [vmem_spec() for _ in range(2)], scratch=rolls, cost=(30 * whole, 3 * whole),
    )(cells_in, strips)
    part_next, part_total = call(
        functools.partial(late_kernel, per_layer, count), [f32(*shape), f32(*shape)],
        [vmem_spec() for _ in range(8)],
        scratch=rolls + [VMEM((edge + reach, LANES), jnp.float32), VMEM((edge + reach, LANES), jnp.float32)],
        cost=(30 * whole, 3 * whole),
    )(cells_in, layers, strips, base, accum, half, pull, rates)
    next_section, accum_out = call(
        final_kernel, [f32(*shape), f32(*shape)],
        [vmem_spec() for _ in range(4 + len(candidates))],
        out_specs=[anywhere, anywhere],
        scratch=[VMEM(faces, jnp.float32)]
        + [VMEM(shape, jnp.float32) for _ in range(2)]
        + [pltpu.SemaphoreType.DMA((2, 2 * faces[0]))],
        cost=(10 * whole, 4 * whole),
    )(routes, half, part_next, part_total, *candidates)
    return (next_section.reshape(state.shape), accum_out.reshape(state.shape))


def direct(columns):
    return 2 < columns <= 8 and columns & (columns - 1) == 0


def exchange(x, d):
    columns = lax.axis_size("gz")
    return lax.ppermute(x, "gz", [(i, i ^ d) for i in range(columns)])


def solution(mesh):
    step = jax.shard_map(
        substep,
        mesh=mesh,
        in_specs=(
            P(None, "gx", ("gy", "gz"), None),
            P(None, "gx", ("gy", "gz"), None),
            P(None, "gx", ("gy", "gz"), None),
            P(),
        ),
        out_specs=(P(None, "gx", ("gy", "gz"), None), P(None, "gx", ("gy", "gz"), None)),
        check_vma=False,
    )
    columns = mesh.shape["gz"]
    if not direct(columns):
        return step
    return step
```

time: 27.5 us -> 24.7 us (0.90)
  Pallas kernels: 8.98 us -> 6.54 us
  waiting for transfers between devices: 6.18 us -> 5.16 us
  local copies, waits for them, and re-layouts: 1.14 us -> 1.8 us
    ppermute x4, waiting for transfers between devices: 6.18 us -> 5.16 us  [exchange(): return lax.ppermute(x, 'gz', [(i, i ^ d) for i in range(columns)])]
    pallas_call x1, Pallas kernels: 2.98 us -> 2.03 us  [substep(): call(functools.partial(late_kernel, per_layer, count), [f32(*shape), f32(...]
    pallas_call x1, Pallas kernels: 0.9 us -> 0.05 us  [substep(): call(functools.partial(pack_ends_kernel, per_layer), [f32(fields, 2 * GHO...]
    ppermute x2, starting transfers between devices: 2.37 us -> 3.12 us  [swap_ends(): return lax.ppermute(ends, axis, [(0, 1), (1, 0)])]
    ppermute x4, starting transfers between devices: 7.96 us -> 7.22 us  [exchange(): return lax.ppermute(x, 'gz', [(i, i ^ d) for i in range(columns)])]
    unnamed x10, local copies, waits for them, and re-layouts: 1.14 us -> 1.8 us
    pallas_call x4 -> x5, Pallas kernels: 5.1 us -> 4.46 us  [the longest x1 1.83 us: substep(): call(functools.partial(early_kernel, per_layer, count), [f32(2 * count, r...]
  transfers between devices with their start and end apart: 6 -> 6, of which waited for: 3 -> 2; matrix products, arithmetic and copies ran while one was open for 0% -> 0% of each run, Pallas kernels for 21% -> 20%
where the time goes in v1:
time: 24.7 us; the launch traced here: 24.6 us
  starting transfers between devices  10.3 us (42%)
  Pallas kernels  6.54 us (26%)
  waiting for transfers between devices  5.16 us (21%)
  local copies, waits for them, and re-layouts  1.8 us (7%)
  between operations  0.73 us (3%)
    ppermute x4, starting transfers between devices, exchange(): return lax.ppermute(x, 'gz', [(i, i ^ d) for i in range(columns)])  7.22 us
    ppermute x4, waiting for transfers between devices, exchange(): return lax.ppermute(x, 'gz', [(i, i ^ d) for i in range(columns)])  5.16 us
    ppermute x2, starting transfers between devices, swap_ends(): return lax.ppermute(ends, axis, [(0, 1), (1, 0)])  3.12 us
    pallas_call x1, Pallas kernels, substep(): call(functools.partial(late_kernel, per_layer, count), [f32(*shape), f32(...  2.03 us
    pallas_call x1, Pallas kernels, substep(): call(functools.partial(early_kernel, per_layer, count), [f32(2 * count, r...  1.83 us
    unnamed x10, local copies, waits for them, and re-layouts  1.8 us
    pallas_call x1, Pallas kernels, substep(): call(final_kernel, [f32(*shape), f32(*shape)], [vmem_spec() for _ in rang...  1.62 us
    pallas_call x1, Pallas kernels, substep(): call(functools.partial(routes_kernel, columns, cross), jax.ShapeDtypeStru...  0.72 us
  transfers between devices with their start and end apart: 6, of which 2 were waited for; matrix products, arithmetic and copies ran while one was open for 0% of the time, Pallas kernels for 20%

profile of v1, /device:TPU:0, one launch (start us, length us, event | category | flops | bytes accessed | tf_op | source)
XLA Modules:
  0.0 24.6 jit_solution(2077711375005743777)
XLA Ops:
  0.6 0.0 copy-start
  0.6 1.1 %copy-done = f32[24,16,1,512]{3,2,1,0:T(1,128)S(1)} copy-done((f32[24,16,1,512]{3,2,1,0:T(1,128)S(1)}, f32[24,16,1,512]{3,2,1,0:T(1,128)}, u32[]{:S(2)}) %copy-start) | copy-done | bytes 786456
  1.8 0.1 shard_map.60
  1.8 0.6 %collective-permute-start = (f32[24,32,128]{2,1,0:T(8,128)S(1)}, f32[24,32,128]{2,1,0:T(8,128)S(1)}, u32[]{:S(2)}, u32[]{:S(2)}) collective-permute-start(f32[24,32,128]{2,1,0:T(8,128)S(1)} %get-tuple-element.11), channel_id=1, source_target_pairs={{0,8},{8,0},{1,9},{9,1},{2,10},{10,2},{3,11},{11,3},{4,12},{12,4},... | collective-permute-start | bytes 1179656 | tf_op jit(solution)/shard_map/ppermute | solution.py:344
  2.4 0.0 copy-start.1
  2.4 2.6 %collective-permute-start.1 = (f32[24,24,128]{2,1,0:T(8,128)S(1)}, f32[24,24,128]{2,1,0:T(8,128)S(1)}, u32[]{:S(2)}, u32[]{:S(2)}) collective-permute-start(f32[24,24,128]{2,1,0:T(8,128)S(1)} %get-tuple-element.13), channel_id=1, source_target_pairs={{0,16},{16,0},{1,17},{17,1},{2,18},{18,2},{3,19},{19,3},{4,20},{20... | collective-permute-start | bytes 884744 | tf_op jit(solution)/shard_map/ppermute | solution.py:344
  4.9 0.3 %shard_map.63.refs_0_ = f32[3,3,32,128]{3,2,1,0:T(8,128)S(1)} custom-call(f32[24,64,128]{2,1,0:T(8,128)S(1)} %bitcast.7), custom_call_target="tpu_custom_call" | custom-call | flops 786432 | bytes 786432 | tf_op jit(solution)/shard_map/pallas_call | solution.py:386
  5.2 2.6 %collective-permute-start.4 = (f32[3,3,32,128]{3,2,1,0:T(8,128)S(1)}, f32[3,3,32,128]{3,2,1,0:T(8,128)S(1)}, u32[]{:S(2)}, u32[]{:S(2)}) collective-permute-start(f32[3,3,32,128]{3,2,1,0:T(8,128)S(1)} %shard_map.63.refs_0_), channel_id=1, source_target_pairs={{0,3},{1,2},{2,1},{3,0},{4,7},{5,6},{6,5},{7,4},{8,11},{9,10},{10,... | collective-permute-start | bytes 442376 | tf_op jit(solution)/shard_map/ppermute | solution.py:445
  7.8 0.4 %collective-permute-start.3 = (f32[3,3,32,128]{3,2,1,0:T(8,128)S(1)}, f32[3,3,32,128]{3,2,1,0:T(8,128)S(1)}, u32[]{:S(2)}, u32[]{:S(2)}) collective-permute-start(f32[3,3,32,128]{3,2,1,0:T(8,128)S(1)} %shard_map.63.refs_0_), channel_id=1, source_target_pairs={{0,2},{1,3},{2,0},{3,1},{4,6},{5,7},{6,4},{7,5},{8,10},{9,11},{10,... | collective-permute-start | bytes 442376 | tf_op jit(solution)/shard_map/ppermute | solution.py:445
  8.3 0.5 %collective-permute-start.2 = (f32[3,3,32,128]{3,2,1,0:T(8,128)S(1)}, f32[3,3,32,128]{3,2,1,0:T(8,128)S(1)}, u32[]{:S(2)}, u32[]{:S(2)}) collective-permute-start(f32[3,3,32,128]{3,2,1,0:T(8,128)S(1)} %shard_map.63.refs_0_), channel_id=1, source_target_pairs={{0,1},{1,0},{2,3},{3,2},{4,5},{5,4},{6,7},{7,6},{8,9},{9,8},{10,11... | collective-permute-start | bytes 442376 | tf_op jit(solution)/shard_map/ppermute | solution.py:445
  8.8 0.0 copy-start.4
  8.8 0.7 %copy-done.4 = s32[8]{0:T(128)S(1)} copy-done((s32[8]{0:T(128)S(1)}, s32[8]{0:T(128)}, u32[]{:S(2)}) %copy-start.4) | copy-done | bytes 56
  9.4 0.7 %shard_map.59.routes_ref = s32[5,8,128]{2,1,0:T(8,128)S(1)} custom-call(s32[8]{0:T(128)S(1)} %copy-done.4, s32[1]{0:T(128)} %bitcast.me_ref), custom_call_target="tpu_custom_call" | custom-call | flops 196608 | bytes 196608 | tf_op jit(solution)/shard_map/pallas_call | solution.py:388
  10.2 0.0 copy-start.2
  10.2 0.0 copy-start.3
  10.2 2.7 %collective-permute-done.4.refs_3_ = f32[3,3,32,128]{3,2,1,0:T(8,128)S(1)} collective-permute-done((f32[3,3,32,128]{3,2,1,0:T(8,128)S(1)}, f32[3,3,32,128]{3,2,1,0:T(8,128)S(1)}, u32[]{:S(2)}, u32[]{:S(2)}) %collective-permute-start.4) | collective-permute-done | bytes 147488 | tf_op jit(solution)/shard_map/ppermute | solution.py:445
  12.9 2.4 %collective-permute-done.3.refs_2_ = f32[3,3,32,128]{3,2,1,0:T(8,128)S(1)} collective-permute-done((f32[3,3,32,128]{3,2,1,0:T(8,128)S(1)}, f32[3,3,32,128]{3,2,1,0:T(8,128)S(1)}, u32[]{:S(2)}, u32[]{:S(2)}) %collective-permute-start.3) | collective-permute-done | bytes 147488 | tf_op jit(solution)/shard_map/ppermute | solution.py:445
  15.3 0.0 collective-permute-done.2.refs_1_
  15.4 3.7 %collective-permute-start.5 = (f32[3,3,32,128]{3,2,1,0:T(8,128)S(1)}, f32[3,3,32,128]{3,2,1,0:T(8,128)S(1)}, u32[]{:S(2)}, u32[]{:S(2)}) collective-permute-start(f32[3,3,32,128]{3,2,1,0:T(8,128)S(1)} %shard_map.64), channel_id=1, source_target_pairs={{0,6},{1,7},{2,4},{3,5},{4,2},{5,3},{6,0},{7,1},{8,14},{9,15},{10,... | collective-permute-start | bytes 442376 | tf_op jit(solution)/shard_map/ppermute | solution.py:445
  19.0 0.0 collective-permute-done.strips_ref
  19.0 0.0 copy-done.1
  19.0 1.8 %shard_map.61 = (f32[12,64,128]{2,1,0:T(8,128)S(1)}, f32[64,128]{1,0:T(8,128)S(1)}, f32[64,128]{1,0:T(8,128)S(1)}) custom-call(f32[24,64,128]{2,1,0:T(8,128)S(1)} %bitcast.8, f32[24,32,128]{2,1,0:T(8,128)S(1)} %collective-permute-done.strips_ref), custom_call_target="tpu_custom_call" | custom-call | flops 23592960 | bytes 2359296 | tf_op jit(solution)/shard_map/pallas_call | solution.py:416
  20.9 0.0 collective-permute-done.1.layers_ref
  20.9 0.0 copy-done.2
  20.9 0.0 copy-done.3
  20.9 2.0 %shard_map.62 = (f32[24,64,128]{2,1,0:T(8,128)S(1)}, f32[24,64,128]{2,1,0:T(8,128)S(1)}) custom-call(f32[24,64,128]{2,1,0:T(8,128)S(1)} %bitcast.9, f32[24,24,128]{2,1,0:T(8,128)S(1)} %collective-permute-done.1.layers_ref, f32[24,32,128]{2,1,0:T(8,128)S(1)} %collective-permute-done.strips_ref, f32[24,64,128]{2,1,0:T(8,128)S(1)} %bitcast.10, ...), custom_call_target="tpu_custom_call" | custom-call | flops 23592960 | bytes 2359296 | tf_op jit(solution)/shard_map/pallas_call | solution.py:421
  22.9 0.0 collective-permute-done.5.refs_0_
  22.9 1.6 %shard_map.65 = (f32[24,64,128]{2,1,0:T(8,128)}, f32[24,64,128]{2,1,0:T(8,128)}) custom-call(s32[5,8,128]{2,1,0:T(8,128)S(1)} %shard_map.59.routes_ref, f32[64,128]{1,0:T(8,128)S(1)} %get-tuple-element.12.half_ref, f32[24,64,128]{2,1,0:T(8,128)S(1)} %get-tuple-element.16.next_ref, f32[24,64,128]{2,1,0:T(8,128)S(1)} %get-tuple-element.17.total_ref, ...), custom_call_target="tpu_custom_call" | custom-call | flops 7864320 | bytes 3145728 | tf_op jit(solution)/shard_map/pallas_call | solution.py:427
  (1 shorter events, 0.0 us)
Async XLA Ops:
  0.6 1.1 %copy-start = (f32[24,16,1,512]{3,2,1,0:T(1,128)S(1)}, f32[24,16,1,512]{3,2,1,0:T(1,128)}, u32[]{:S(2)}) copy-start(f32[24,16,1,512]{3,2,1,0:T(1,128)} %param.4) | copy-start | bytes 2359300
  1.8 17.2 %collective-permute-start = (f32[24,32,128]{2,1,0:T(8,128)S(1)}, f32[24,32,128]{2,1,0:T(8,128)S(1)}, u32[]{:S(2)}, u32[]{:S(2)}) collective-permute-start(f32[24,32,128]{2,1,0:T(8,128)S(1)} %get-tuple-element.11), channel_id=1, source_target_pairs={{0,8},{8,0},{1,9},{9,1},{2,10},{10,2},{3,11},{11,3},{4,12},{12,4},... | collective-permute-start | bytes 1179656 | tf_op jit(solution)/shard_map/ppermute | solution.py:344
  2.4 16.7 %copy-start.1 = (f32[24,16,1,512]{3,2,1,0:T(1,128)S(1)}, f32[24,16,1,512]{3,2,1,0:T(1,128)}, u32[]{:S(2)}) copy-start(f32[24,16,1,512]{3,2,1,0:T(1,128)} %param.4) | copy-start | bytes 2359300
  2.4 18.5 %collective-permute-start.1 = (f32[24,24,128]{2,1,0:T(8,128)S(1)}, f32[24,24,128]{2,1,0:T(8,128)S(1)}, u32[]{:S(2)}, u32[]{:S(2)}) collective-permute-start(f32[24,24,128]{2,1,0:T(8,128)S(1)} %get-tuple-element.13), channel_id=1, source_target_pairs={{0,16},{16,0},{1,17},{17,1},{2,18},{18,2},{3,19},{19,3},{4,20},{20... | collective-permute-start | bytes 884744 | tf_op jit(solution)/shard_map/ppermute | solution.py:344
  5.2 7.7 %collective-permute-start.4 = (f32[3,3,32,128]{3,2,1,0:T(8,128)S(1)}, f32[3,3,32,128]{3,2,1,0:T(8,128)S(1)}, u32[]{:S(2)}, u32[]{:S(2)}) collective-permute-start(f32[3,3,32,128]{3,2,1,0:T(8,128)S(1)} %shard_map.63.refs_0_), channel_id=1, source_target_pairs={{0,3},{1,2},{2,1},{3,0},{4,7},{5,6},{6,5},{7,4},{8,11},{9,10},{10,... | collective-permute-start | bytes 442376 | tf_op jit(solution)/shard_map/ppermute | solution.py:445
  7.8 7.5 %collective-permute-start.3 = (f32[3,3,32,128]{3,2,1,0:T(8,128)S(1)}, f32[3,3,32,128]{3,2,1,0:T(8,128)S(1)}, u32[]{:S(2)}, u32[]{:S(2)}) collective-permute-start(f32[3,3,32,128]{3,2,1,0:T(8,128)S(1)} %shard_map.63.refs_0_), channel_id=1, source_target_pairs={{0,2},{1,3},{2,0},{3,1},{4,6},{5,7},{6,4},{7,5},{8,10},{9,11},{10,... | collective-permute-start | bytes 442376 | tf_op jit(solution)/shard_map/ppermute | solution.py:445
  8.3 7.1 %collective-permute-start.2 = (f32[3,3,32,128]{3,2,1,0:T(8,128)S(1)}, f32[3,3,32,128]{3,2,1,0:T(8,128)S(1)}, u32[]{:S(2)}, u32[]{:S(2)}) collective-permute-start(f32[3,3,32,128]{3,2,1,0:T(8,128)S(1)} %shard_map.63.refs_0_), channel_id=1, source_target_pairs={{0,1},{1,0},{2,3},{3,2},{4,5},{5,4},{6,7},{7,6},{8,9},{9,8},{10,11... | collective-permute-start | bytes 442376 | tf_op jit(solution)/shard_map/ppermute | solution.py:445
  8.8 0.7 %copy-start.4 = (s32[8]{0:T(128)S(1)}, s32[8]{0:T(128)}, u32[]{:S(2)}) copy-start(s32[8]{0:T(128)} %owner_ref.1) | copy-start | bytes 100
  10.2 10.7 %copy-start.2 = (f32[24,16,1,512]{3,2,1,0:T(1,128)S(1)}, f32[24,16,1,512]{3,2,1,0:T(1,128)}, u32[]{:S(2)}) copy-start(f32[24,16,1,512]{3,2,1,0:T(1,128)} %param.5) | copy-start | bytes 2359300
  10.2 10.7 %copy-start.3 = (f32[24,16,1,512]{3,2,1,0:T(1,128)S(1)}, f32[24,16,1,512]{3,2,1,0:T(1,128)}, u32[]{:S(2)}) copy-start(f32[24,16,1,512]{3,2,1,0:T(1,128)} %param.6) | copy-start | bytes 2359300
  15.4 7.6 %collective-permute-start.5 = (f32[3,3,32,128]{3,2,1,0:T(8,128)S(1)}, f32[3,3,32,128]{3,2,1,0:T(8,128)S(1)}, u32[]{:S(2)}, u32[]{:S(2)}) collective-permute-start(f32[3,3,32,128]{3,2,1,0:T(8,128)S(1)} %shard_map.64), channel_id=1, source_target_pairs={{0,6},{1,7},{2,4},{3,5},{4,2},{5,3},{6,0},{7,1},{8,14},{9,15},{10,... | collective-permute-start | bytes 442376 | tf_op jit(solution)/shard_map/ppermute | solution.py:445
